TPU v7x, 32 devices: a whole 2x2x4 slice. The times are simulated.
32 devices in a mesh: grp: 4 (over z), sub: 4 (over y, x), rep: 2 (over core).
Axes of the slice: x: 2, y: 2, z: 4, core: 2. Of those that a mesh axis runs over, the one named last changes fastest.
Arguments:
- starting_concentration_per_run: float32 [4, 8, 256, 512], P('grp', None, 'sub', 'rep'), may hold values from -6 to 6
- diffusivity: float32 [256, 512], P('sub', 'rep'), may hold values from 0.02 to 0.12
- run_layer_stability_number: float32 [4, 8], P('grp'), may hold values from 0.05 to 0.4
- observed: float32 [256, 4, 128], P(('sub', 'grp'), 'rep'), may hold values from -6 to 6
- slot_error_variance: float32 [256, 4, 128], P(('sub', 'grp'), 'rep'), may hold values from 0.25 to 4
- sensor_target_site: int32 [256, 4, 128], P(('sub', 'grp'), 'rep'), may hold values from 0 to 1023
- patch_live_count: int32 [256, 4], P(('sub', 'grp'), 'rep'), may hold values from 1 to 128, as said below
Outputs:
- analysis: float32 [4, 8, 256, 512], P('grp', None, 'sub', 'rep')
Inputs may be any that keep to these rules, and one draw needn't show every extreme that they name: Slots below patch_live_count of a patch are live, the rest are unused; some patch has all 128 slots live. `sensor_target_site`: A slot observes the cell level * 128 + column of its own patch.
All inputs are finite; a program needn't handle non-finite values.
Results may differ from a plain program's by a relative error of at most 0.0003.
Values sent between devices are 32-bit elements; how exact they have to be, the bound alone decides.
A program may use at most 64 MiB of HBM per device.

v0:
```python
import jax
import jax.numpy as jnp
from jax import lax
from jax.sharding import PartitionSpec as P

PATCH = 128
STEPS = 4
NS_ITERS = 4


HIGHEST = lax.Precision.HIGHEST


def extended(x, sides, width):
    for axis, dim in sides:
        devices, length = (lax.axis_size(axis), x.shape[dim])
        up = [(i, (i + 1) % devices) for i in range(devices - 1)]
        down = [(j, i) for i, j in up]
        last = lax.slice_in_dim(x, length - width, length, axis=dim)
        initial = lax.slice_in_dim(x, 0, width, axis=dim)
        before = lax.ppermute(last, axis, up)
        after = lax.ppermute(initial, axis, down)
        x = jnp.concatenate([before, x, after], axis=dim)
    return x


def advance(padded, diffusivity, member_wind):
    centre = padded[..., 1:-1, 1:-1]
    northern = padded[..., :-2, 1:-1]
    southern = padded[..., 2:, 1:-1]
    western = padded[..., 1:-1, :-2]
    easterly_side = padded[..., 1:-1, 2:]
    spread = northern + southern + (western + easterly_side) - 4.0 * centre
    return centre + diffusivity * spread - member_wind * (centre - western)


def analyse(background, sampled, observed, slot_error_variance, patch_live_count):
    members = background.shape[1]
    slots = observed.shape[-1]
    centre_mean = jnp.mean(background, axis=1, keepdims=True)
    perturbed = background - centre_mean
    sampled_mean = jnp.mean(sampled, axis=1, keepdims=True)
    sampled_pert = sampled - sampled_mean
    live_slot = jnp.arange(slots)[None, :] < patch_live_count[:, None]
    precision_obs = jnp.where(live_slot, 1.0 / slot_error_variance, 0.0 * slot_error_variance)
    innovation = observed - sampled_mean[:, 0, :]
    weighted = sampled_pert * precision_obs[:, None, :]
    identity = jnp.eye(members, dtype=background.dtype)
    system = (
        jnp.einsum("pms,pns->pmn", weighted, sampled_pert, precision=HIGHEST)
        + (members - 1.0) * identity
    )
    source_term = jnp.einsum("pms,ps->pm", weighted, innovation, precision=HIGHEST)
    factor = jnp.linalg.cholesky(system)
    halfway = lax.linalg.triangular_solve(
        factor, source_term[:, :, None], left_side=True, lower=True
    )
    mean_weight = lax.linalg.triangular_solve(
        factor, halfway, left_side=True, lower=True, transpose_a=True
    )[:, :, 0]
    norm_scale = jnp.sqrt(jnp.sum(system * system, axis=(1, 2)))
    iterate = system / norm_scale[:, None, None]
    inverse_root = jnp.broadcast_to(identity, system.shape)
    for sweep in range(NS_ITERS):
        update = 1.5 * identity - 0.5 * jnp.einsum(
            "pij,pjk->pik", inverse_root, iterate, precision=HIGHEST
        )
        iterate = jnp.einsum("pij,pjk->pik", iterate, update, precision=HIGHEST)
        inverse_root = jnp.einsum("pij,pjk->pik", update, inverse_root, precision=HIGHEST)
    spread_weight = inverse_root * jnp.sqrt((members - 1.0) / norm_scale)[:, None, None]
    combined = spread_weight + mean_weight[:, :, None]
    return centre_mean + jnp.einsum("pki,pkc->pic", combined, perturbed, precision=HIGHEST)


def on_device(
    starting_concentration_per_run,
    diffusivity,
    run_layer_stability_number,
    observed,
    slot_error_variance,
    sensor_target_site,
    patch_live_count,
):
    member_wind = run_layer_stability_number[:, :, None, None]
    present_state = starting_concentration_per_run
    for stepno in range(STEPS):
        padded = extended(present_state, (("sub", 2), ("rep", 3)), 1)
        present_state = advance(padded, diffusivity, member_wind)
    gathered = lax.all_to_all(present_state, "grp", split_axis=2, concat_axis=0, tiled=True)
    members, levels, row_group, row_width = gathered.shape
    patches = row_width // PATCH
    background = jnp.transpose(
        gathered.reshape(members, levels, row_group, patches, PATCH), (2, 3, 0, 1, 4)
    ).reshape(row_group * patches, members, levels * PATCH)
    slots = observed.shape[-1]
    cell_flat = sensor_target_site.reshape(-1, slots)
    selector = (cell_flat[:, :, None] == jnp.arange(levels * PATCH)[None, None, :]).astype(
        jnp.float32
    )
    sampled = jnp.einsum("pmc,psc->pms", background, selector, precision=HIGHEST)
    result = analyse(
        background,
        sampled,
        observed.reshape(-1, slots),
        slot_error_variance.reshape(-1, slots),
        patch_live_count.reshape(-1),
    )
    returned = jnp.transpose(
        result.reshape(row_group, patches, members, levels, PATCH), (2, 3, 0, 1, 4)
    ).reshape(members, levels, row_group, row_width)
    return lax.all_to_all(returned, "grp", split_axis=0, concat_axis=2, tiled=True)


def solution(mesh):
    in_specs = (
        P("grp", None, "sub", "rep"),
        P("sub", "rep"),
        P("grp", None),
        P(("sub", "grp"), "rep", None),
        P(("sub", "grp"), "rep", None),
        P(("sub", "grp"), "rep", None),
        P(("sub", "grp"), "rep"),
    )
    out_specs = P("grp", None, "sub", "rep")
    return jax.shard_map(
        on_device, mesh=mesh, in_specs=in_specs, out_specs=out_specs, check_vma=False
    )
```

profile of v0, /device:TPU:0, one launch (start us, length us, event | category | flops | bytes accessed | tf_op | source)
XLA Modules:
  0.0 129.2 jit_solution(15507123286663348765)
XLA Ops:
  0.0 1.4 %copy.69 = f32[1,8,64,256]{3,1,0,2:T(8,128)S(1)} copy(f32[1,8,64,256]{3,2,1,0:T(8,128)} %param.7) | data formatting | bytes 1048576 | tf_op args[0]
  1.4 4.9 %collective-permute-start = (f32[1,8,1,256]{3,1,0,2:T(8,128)S(1)}, f32[1,8,1,256]{3,1,0,2:T(8,128)S(1)}, u32[]{:S(2)}, u32[]{:S(2)}) collective-permute-start(f32[1,8,1,256]{3,1,0,2:T(8,128)S(1)} %get-tuple-element.20), channel_id=1, source_target_pairs={{0,2},{2,4},{4,6},{1,3},{3,5},{5,7},{8,10},{10,12},{12,14},{9,11},... | collective-permute-start | bytes 24584 | tf_op jit(solution)/shard_map/ppermute | solution.py:21
  6.3 1.3 %collective-permute-start.1 = (f32[1,8,1,256]{3,1,0,2:T(8,128)S(1)}, f32[1,8,1,256]{3,1,0,2:T(8,128)S(1)}, u32[]{:S(2)}, u32[]{:S(2)}) collective-permute-start(f32[1,8,1,256]{3,1,0,2:T(8,128)S(1)} %get-tuple-element.19), channel_id=1, source_target_pairs={{2,0},{4,2},{6,4},{3,1},{5,3},{7,5},{10,8},{12,10},{14,12},{11,9},... | collective-permute-start | bytes 24584 | tf_op jit(solution)/shard_map/ppermute | solution.py:22
  8.0 3.9 %collective-permute-done.1 = f32[1,8,1,256]{3,1,0,2:T(8,128)S(1)} collective-permute-done((f32[1,8,1,256]{3,1,0,2:T(8,128)S(1)}, f32[1,8,1,256]{3,1,0,2:T(8,128)S(1)}, u32[]{:S(2)}, u32[]{:S(2)}) %collective-permute-start.1) | collective-permute-done | bytes 8224 | tf_op jit(solution)/shard_map/ppermute | solution.py:22
  12.0 1.3 %collective-permute-start.2 = (f32[1,8,66,1]{3,1,0,2:T(8,128)S(1)}, f32[1,8,66,1]{3,1,0,2:T(8,128)S(1)}, u32[]{:S(2)}, u32[]{:S(2)}) collective-permute-start(f32[1,8,66,1]{3,1,0,2:T(8,128)S(1)} %get-tuple-element.11), channel_id=1, source_target_pairs={{0,1},{2,3},{4,5},{6,7},{8,9},{10,11},{12,13},{14,15},{16,17},{18,... | collective-permute-start | bytes 6344 | tf_op jit(solution)/shard_map/ppermute | solution.py:21
  13.3 1.3 %collective-permute-start.3 = (f32[1,8,66,1]{3,1,0,2:T(8,128)S(1)}, f32[1,8,66,1]{3,1,0,2:T(8,128)S(1)}, u32[]{:S(2)}, u32[]{:S(2)}) collective-permute-start(f32[1,8,66,1]{3,1,0,2:T(8,128)S(1)} %get-tuple-element.12), channel_id=1, source_target_pairs={{1,0},{3,2},{5,4},{7,6},{9,8},{11,10},{13,12},{15,14},{17,16},{19,... | collective-permute-start | bytes 6344 | tf_op jit(solution)/shard_map/ppermute | solution.py:22
  14.6 2.1 %collective-permute-done.3 = f32[1,8,66,1]{3,1,0,2:T(8,128)S(1)} collective-permute-done((f32[1,8,66,1]{3,1,0,2:T(8,128)S(1)}, f32[1,8,66,1]{3,1,0,2:T(8,128)S(1)}, u32[]{:S(2)}, u32[]{:S(2)}) %collective-permute-start.3) | collective-permute-done | bytes 2144 | tf_op jit(solution)/shard_map/ppermute | solution.py:22
  17.2 4.3 %collective-permute-start.4 = (f32[1,8,1,256]{3,1,0,2:T(8,128)S(1)}, f32[1,8,1,256]{3,1,0,2:T(8,128)S(1)}, u32[]{:S(2)}, u32[]{:S(2)}) collective-permute-start(f32[1,8,1,256]{3,1,0,2:T(8,128)S(1)} %get-tuple-element.17), channel_id=1, source_target_pairs={{0,2},{2,4},{4,6},{1,3},{3,5},{5,7},{8,10},{10,12},{12,14},{9,11},... | collective-permute-start | bytes 24584 | tf_op jit(solution)/shard_map/ppermute | solution.py:21
  21.5 1.3 %collective-permute-start.5 = (f32[1,8,1,256]{3,1,0,2:T(8,128)S(1)}, f32[1,8,1,256]{3,1,0,2:T(8,128)S(1)}, u32[]{:S(2)}, u32[]{:S(2)}) collective-permute-start(f32[1,8,1,256]{3,1,0,2:T(8,128)S(1)} %get-tuple-element.18), channel_id=1, source_target_pairs={{2,0},{4,2},{6,4},{3,1},{5,3},{7,5},{10,8},{12,10},{14,12},{11,9},... | collective-permute-start | bytes 24584 | tf_op jit(solution)/shard_map/ppermute | solution.py:22
  22.9 4.2 %collective-permute-done.5 = f32[1,8,1,256]{3,1,0,2:T(8,128)S(1)} collective-permute-done((f32[1,8,1,256]{3,1,0,2:T(8,128)S(1)}, f32[1,8,1,256]{3,1,0,2:T(8,128)S(1)}, u32[]{:S(2)}, u32[]{:S(2)}) %collective-permute-start.5) | collective-permute-done | bytes 8224 | tf_op jit(solution)/shard_map/ppermute | solution.py:22
  27.2 1.3 %collective-permute-start.6 = (f32[1,8,66,1]{3,1,0,2:T(8,128)S(1)}, f32[1,8,66,1]{3,1,0,2:T(8,128)S(1)}, u32[]{:S(2)}, u32[]{:S(2)}) collective-permute-start(f32[1,8,66,1]{3,1,0,2:T(8,128)S(1)} %get-tuple-element.9), channel_id=1, source_target_pairs={{0,1},{2,3},{4,5},{6,7},{8,9},{10,11},{12,13},{14,15},{16,17},{18,... | collective-permute-start | bytes 6344 | tf_op jit(solution)/shard_map/ppermute | solution.py:21
  28.5 1.3 %collective-permute-start.7 = (f32[1,8,66,1]{3,1,0,2:T(8,128)S(1)}, f32[1,8,66,1]{3,1,0,2:T(8,128)S(1)}, u32[]{:S(2)}, u32[]{:S(2)}) collective-permute-start(f32[1,8,66,1]{3,1,0,2:T(8,128)S(1)} %get-tuple-element.10), channel_id=1, source_target_pairs={{1,0},{3,2},{5,4},{7,6},{9,8},{11,10},{13,12},{15,14},{17,16},{19,... | collective-permute-start | bytes 6344 | tf_op jit(solution)/shard_map/ppermute | solution.py:22
  29.9 2.1 %collective-permute-done.7 = f32[1,8,66,1]{3,1,0,2:T(8,128)S(1)} collective-permute-done((f32[1,8,66,1]{3,1,0,2:T(8,128)S(1)}, f32[1,8,66,1]{3,1,0,2:T(8,128)S(1)}, u32[]{:S(2)}, u32[]{:S(2)}) %collective-permute-start.7) | collective-permute-done | bytes 2144 | tf_op jit(solution)/shard_map/ppermute | solution.py:22
  32.4 3.4 %collective-permute-start.8 = (f32[1,8,1,256]{3,1,0,2:T(8,128)S(1)}, f32[1,8,1,256]{3,1,0,2:T(8,128)S(1)}, u32[]{:S(2)}, u32[]{:S(2)}) collective-permute-start(f32[1,8,1,256]{3,1,0,2:T(8,128)S(1)} %get-tuple-element.15), channel_id=1, source_target_pairs={{0,2},{2,4},{4,6},{1,3},{3,5},{5,7},{8,10},{10,12},{12,14},{9,11},... | collective-permute-start | bytes 24584 | tf_op jit(solution)/shard_map/ppermute | solution.py:21
  35.8 1.3 %collective-permute-start.9 = (f32[1,8,1,256]{3,1,0,2:T(8,128)S(1)}, f32[1,8,1,256]{3,1,0,2:T(8,128)S(1)}, u32[]{:S(2)}, u32[]{:S(2)}) collective-permute-start(f32[1,8,1,256]{3,1,0,2:T(8,128)S(1)} %get-tuple-element.16), channel_id=1, source_target_pairs={{2,0},{4,2},{6,4},{3,1},{5,3},{7,5},{10,8},{12,10},{14,12},{11,9},... | collective-permute-start | bytes 24584 | tf_op jit(solution)/shard_map/ppermute | solution.py:22
  37.2 4.2 %collective-permute-done.9 = f32[1,8,1,256]{3,1,0,2:T(8,128)S(1)} collective-permute-done((f32[1,8,1,256]{3,1,0,2:T(8,128)S(1)}, f32[1,8,1,256]{3,1,0,2:T(8,128)S(1)}, u32[]{:S(2)}, u32[]{:S(2)}) %collective-permute-start.9) | collective-permute-done | bytes 8224 | tf_op jit(solution)/shard_map/ppermute | solution.py:22
  41.5 1.3 %collective-permute-start.10 = (f32[1,8,66,1]{3,1,0,2:T(8,128)S(1)}, f32[1,8,66,1]{3,1,0,2:T(8,128)S(1)}, u32[]{:S(2)}, u32[]{:S(2)}) collective-permute-start(f32[1,8,66,1]{3,1,0,2:T(8,128)S(1)} %get-tuple-element.7), channel_id=1, source_target_pairs={{0,1},{2,3},{4,5},{6,7},{8,9},{10,11},{12,13},{14,15},{16,17},{18,... | collective-permute-start | bytes 6344 | tf_op jit(solution)/shard_map/ppermute | solution.py:21
  42.9 1.3 %collective-permute-start.11 = (f32[1,8,66,1]{3,1,0,2:T(8,128)S(1)}, f32[1,8,66,1]{3,1,0,2:T(8,128)S(1)}, u32[]{:S(2)}, u32[]{:S(2)}) collective-permute-start(f32[1,8,66,1]{3,1,0,2:T(8,128)S(1)} %get-tuple-element.8), channel_id=1, source_target_pairs={{1,0},{3,2},{5,4},{7,6},{9,8},{11,10},{13,12},{15,14},{17,16},{19,... | collective-permute-start | bytes 6344 | tf_op jit(solution)/shard_map/ppermute | solution.py:22
  44.2 2.1 %collective-permute-done.11 = f32[1,8,66,1]{3,1,0,2:T(8,128)S(1)} collective-permute-done((f32[1,8,66,1]{3,1,0,2:T(8,128)S(1)}, f32[1,8,66,1]{3,1,0,2:T(8,128)S(1)}, u32[]{:S(2)}, u32[]{:S(2)}) %collective-permute-start.11) | collective-permute-done | bytes 2144 | tf_op jit(solution)/shard_map/ppermute | solution.py:22
  46.7 2.8 %collective-permute-start.12 = (f32[1,8,1,256]{3,1,0,2:T(8,128)S(1)}, f32[1,8,1,256]{3,1,0,2:T(8,128)S(1)}, u32[]{:S(2)}, u32[]{:S(2)}) collective-permute-start(f32[1,8,1,256]{3,1,0,2:T(8,128)S(1)} %get-tuple-element.13), channel_id=1, source_target_pairs={{0,2},{2,4},{4,6},{1,3},{3,5},{5,7},{8,10},{10,12},{12,14},{9,11},... | collective-permute-start | bytes 24584 | tf_op jit(solution)/shard_map/ppermute | solution.py:21
  49.6 1.3 %collective-permute-start.13 = (f32[1,8,1,256]{3,1,0,2:T(8,128)S(1)}, f32[1,8,1,256]{3,1,0,2:T(8,128)S(1)}, u32[]{:S(2)}, u32[]{:S(2)}) collective-permute-start(f32[1,8,1,256]{3,1,0,2:T(8,128)S(1)} %get-tuple-element.14), channel_id=1, source_target_pairs={{2,0},{4,2},{6,4},{3,1},{5,3},{7,5},{10,8},{12,10},{14,12},{11,9},... | collective-permute-start | bytes 24584 | tf_op jit(solution)/shard_map/ppermute | solution.py:22
  50.9 4.2 %collective-permute-done.13 = f32[1,8,1,256]{3,1,0,2:T(8,128)S(1)} collective-permute-done((f32[1,8,1,256]{3,1,0,2:T(8,128)S(1)}, f32[1,8,1,256]{3,1,0,2:T(8,128)S(1)}, u32[]{:S(2)}, u32[]{:S(2)}) %collective-permute-start.13) | collective-permute-done | bytes 8224 | tf_op jit(solution)/shard_map/ppermute | solution.py:22
  55.3 1.3 %collective-permute-start.14 = (f32[1,8,66,1]{3,1,0,2:T(8,128)S(1)}, f32[1,8,66,1]{3,1,0,2:T(8,128)S(1)}, u32[]{:S(2)}, u32[]{:S(2)}) collective-permute-start(f32[1,8,66,1]{3,1,0,2:T(8,128)S(1)} %get-tuple-element.5), channel_id=1, source_target_pairs={{0,1},{2,3},{4,5},{6,7},{8,9},{10,11},{12,13},{14,15},{16,17},{18,... | collective-permute-start | bytes 6344 | tf_op jit(solution)/shard_map/ppermute | solution.py:21
  56.6 1.3 %collective-permute-start.15 = (f32[1,8,66,1]{3,1,0,2:T(8,128)S(1)}, f32[1,8,66,1]{3,1,0,2:T(8,128)S(1)}, u32[]{:S(2)}, u32[]{:S(2)}) collective-permute-start(f32[1,8,66,1]{3,1,0,2:T(8,128)S(1)} %get-tuple-element.6), channel_id=1, source_target_pairs={{1,0},{3,2},{5,4},{7,6},{9,8},{11,10},{13,12},{15,14},{17,16},{19,... | collective-permute-start | bytes 6344 | tf_op jit(solution)/shard_map/ppermute | solution.py:22
  57.9 2.1 %collective-permute-done.15 = f32[1,8,66,1]{3,1,0,2:T(8,128)S(1)} collective-permute-done((f32[1,8,66,1]{3,1,0,2:T(8,128)S(1)}, f32[1,8,66,1]{3,1,0,2:T(8,128)S(1)}, u32[]{:S(2)}, u32[]{:S(2)}) %collective-permute-start.15) | collective-permute-done | bytes 2144 | tf_op jit(solution)/shard_map/ppermute | solution.py:22
  60.0 1.2 fusion.12
  61.2 5.0 %all-to-all-start = ((f32[1,8,64,256]{3,1,0,2:T(8,128)}), f32[1,8,64,256]{3,1,0,2:T(8,128)S(1)}, u32[]{:S(2)}, u32[]{:S(2)}) async-start(f32[1,8,64,256]{3,1,0,2:T(8,128)} %fusion.12), calls=%async_computation | async-start | bytes 1048576 | tf_op jit(solution)/shard_map/all_to_all | solution.py:89
  66.5 14.5 %all-to-all-done = f32[1,8,64,256]{3,1,0,2:T(8,128)S(1)} async-done(((f32[1,8,64,256]{3,1,0,2:T(8,128)}), f32[1,8,64,256]{3,1,0,2:T(8,128)S(1)}, u32[]{:S(2)}, u32[]{:S(2)}) %all-to-all-start) | async-done | bytes 524320 | tf_op jit(solution)/shard_map/all_to_all | solution.py:89
  82.5 7.6 %fusion.71 = (f32[32,128]{1,0:T(8,128)S(1)}, f32[32,4,128]{2,1,0:T(4,128)S(1)}) fusion(f32[32,4,1024]{2,1,0:T(4,128)S(1)} %reshape.113, s32[32,128]{1,0:T(8,128)S(1)} %bitcast.98), kind=kOutput, calls=%fused_computation.135 | convolution fusion | flops 205533184 | bytes 622592 | tf_op jit(solution)/shard_map/pmc,psc->pms/dot_general | solution.py:100
  95.1 12.1 %custom-call.9 = f32[32,4,4]{2,1,0:T(4,128)S(1)} custom-call(f32[32,4,4]{2,1,0:T(4,128)S(1)} %get-tuple-element.21), custom_call_target="Cholesky" | custom-call | tf_op jit(solution)/shard_map/jit(cholesky)/cholesky | solution.py:54
  109.6 1.2 convolution_add_fusion
  111.9 16.4 %all_to_all.33 = f32[4,8,16,256]{3,2,1,0:T(8,128)S(1)} all-to-all(f32[4,8,16,256]{3,2,1,0:T(8,128)S(1)} %reshape.116), channel_id=1, replica_groups=mesh['grp'=4,'sub'=4,'rep'=2] {'grp'}, dimensions={0} | all-to-all | bytes 1048576 | tf_op jit(solution)/shard_map/all_to_all | solution.py:111
  (83 shorter events, 13.2 us)
Async XLA Ops:
  0.0 7.7 %copy-start = (f32[1,8,64,256]{3,2,1,0:T(8,128)S(1)}, f32[1,8,64,256]{3,2,1,0:T(8,128)}, u32[]{:S(2)}) copy-start(f32[1,8,64,256]{3,2,1,0:T(8,128)} %param.7) | copy-start | bytes 1572868
  1.4 6.2 %collective-permute-start = (f32[1,8,1,256]{3,1,0,2:T(8,128)S(1)}, f32[1,8,1,256]{3,1,0,2:T(8,128)S(1)}, u32[]{:S(2)}, u32[]{:S(2)}) collective-permute-start(f32[1,8,1,256]{3,1,0,2:T(8,128)S(1)} %get-tuple-element.20), channel_id=1, source_target_pairs={{0,2},{2,4},{4,6},{1,3},{3,5},{5,7},{8,10},{10,12},{12,14},{9,11},... | collective-permute-start | bytes 24584 | tf_op jit(solution)/shard_map/ppermute | solution.py:21
  6.3 5.5 %collective-permute-start.1 = (f32[1,8,1,256]{3,1,0,2:T(8,128)S(1)}, f32[1,8,1,256]{3,1,0,2:T(8,128)S(1)}, u32[]{:S(2)}, u32[]{:S(2)}) collective-permute-start(f32[1,8,1,256]{3,1,0,2:T(8,128)S(1)} %get-tuple-element.19), channel_id=1, source_target_pairs={{2,0},{4,2},{6,4},{3,1},{5,3},{7,5},{10,8},{12,10},{14,12},{11,9},... | collective-permute-start | bytes 24584 | tf_op jit(solution)/shard_map/ppermute | solution.py:22
  11.9 4.9 %copy-start.1 = (f32[64,256]{1,0:T(8,128)S(1)}, f32[64,256]{1,0:T(8,128)}, u32[]{:S(2)}) copy-start(f32[64,256]{1,0:T(8,128)} %param.8) | copy-start | bytes 196612
  11.9 4.9 %copy-start.4 = (f32[1,8]{1,0:T(1,128)S(1)}, f32[1,8]{1,0:T(1,128)}, u32[]{:S(2)}) copy-start(f32[1,8]{1,0:T(1,128)} %param.9) | copy-start | bytes 100
  12.0 2.6 %collective-permute-start.2 = (f32[1,8,66,1]{3,1,0,2:T(8,128)S(1)}, f32[1,8,66,1]{3,1,0,2:T(8,128)S(1)}, u32[]{:S(2)}, u32[]{:S(2)}) collective-permute-start(f32[1,8,66,1]{3,1,0,2:T(8,128)S(1)} %get-tuple-element.11), channel_id=1, source_target_pairs={{0,1},{2,3},{4,5},{6,7},{8,9},{10,11},{12,13},{14,15},{16,17},{18,... | collective-permute-start | bytes 6344 | tf_op jit(solution)/shard_map/ppermute | solution.py:21
  13.3 3.4 %collective-permute-start.3 = (f32[1,8,66,1]{3,1,0,2:T(8,128)S(1)}, f32[1,8,66,1]{3,1,0,2:T(8,128)S(1)}, u32[]{:S(2)}, u32[]{:S(2)}) collective-permute-start(f32[1,8,66,1]{3,1,0,2:T(8,128)S(1)} %get-tuple-element.12), channel_id=1, source_target_pairs={{1,0},{3,2},{5,4},{7,6},{9,8},{11,10},{13,12},{15,14},{17,16},{19,... | collective-permute-start | bytes 6344 | tf_op jit(solution)/shard_map/ppermute | solution.py:22
  17.2 5.7 %collective-permute-start.4 = (f32[1,8,1,256]{3,1,0,2:T(8,128)S(1)}, f32[1,8,1,256]{3,1,0,2:T(8,128)S(1)}, u32[]{:S(2)}, u32[]{:S(2)}) collective-permute-start(f32[1,8,1,256]{3,1,0,2:T(8,128)S(1)} %get-tuple-element.17), channel_id=1, source_target_pairs={{0,2},{2,4},{4,6},{1,3},{3,5},{5,7},{8,10},{10,12},{12,14},{9,11},... | collective-permute-start | bytes 24584 | tf_op jit(solution)/shard_map/ppermute | solution.py:21
  21.5 5.5 %collective-permute-start.5 = (f32[1,8,1,256]{3,1,0,2:T(8,128)S(1)}, f32[1,8,1,256]{3,1,0,2:T(8,128)S(1)}, u32[]{:S(2)}, u32[]{:S(2)}) collective-permute-start(f32[1,8,1,256]{3,1,0,2:T(8,128)S(1)} %get-tuple-element.18), channel_id=1, source_target_pairs={{2,0},{4,2},{6,4},{3,1},{5,3},{7,5},{10,8},{12,10},{14,12},{11,9},... | collective-permute-start | bytes 24584 | tf_op jit(solution)/shard_map/ppermute | solution.py:22
  27.2 2.6 %collective-permute-start.6 = (f32[1,8,66,1]{3,1,0,2:T(8,128)S(1)}, f32[1,8,66,1]{3,1,0,2:T(8,128)S(1)}, u32[]{:S(2)}, u32[]{:S(2)}) collective-permute-start(f32[1,8,66,1]{3,1,0,2:T(8,128)S(1)} %get-tuple-element.9), channel_id=1, source_target_pairs={{0,1},{2,3},{4,5},{6,7},{8,9},{10,11},{12,13},{14,15},{16,17},{18,... | collective-permute-start | bytes 6344 | tf_op jit(solution)/shard_map/ppermute | solution.py:21
  28.5 3.4 %collective-permute-start.7 = (f32[1,8,66,1]{3,1,0,2:T(8,128)S(1)}, f32[1,8,66,1]{3,1,0,2:T(8,128)S(1)}, u32[]{:S(2)}, u32[]{:S(2)}) collective-permute-start(f32[1,8,66,1]{3,1,0,2:T(8,128)S(1)} %get-tuple-element.10), channel_id=1, source_target_pairs={{1,0},{3,2},{5,4},{7,6},{9,8},{11,10},{13,12},{15,14},{17,16},{19,... | collective-permute-start | bytes 6344 | tf_op jit(solution)/shard_map/ppermute | solution.py:22
  32.4 4.8 %collective-permute-start.8 = (f32[1,8,1,256]{3,1,0,2:T(8,128)S(1)}, f32[1,8,1,256]{3,1,0,2:T(8,128)S(1)}, u32[]{:S(2)}, u32[]{:S(2)}) collective-permute-start(f32[1,8,1,256]{3,1,0,2:T(8,128)S(1)} %get-tuple-element.15), channel_id=1, source_target_pairs={{0,2},{2,4},{4,6},{1,3},{3,5},{5,7},{8,10},{10,12},{12,14},{9,11},... | collective-permute-start | bytes 24584 | tf_op jit(solution)/shard_map/ppermute | solution.py:21
  35.8 5.5 %collective-permute-start.9 = (f32[1,8,1,256]{3,1,0,2:T(8,128)S(1)}, f32[1,8,1,256]{3,1,0,2:T(8,128)S(1)}, u32[]{:S(2)}, u32[]{:S(2)}) collective-permute-start(f32[1,8,1,256]{3,1,0,2:T(8,128)S(1)} %get-tuple-element.16), channel_id=1, source_target_pairs={{2,0},{4,2},{6,4},{3,1},{5,3},{7,5},{10,8},{12,10},{14,12},{11,9},... | collective-permute-start | bytes 24584 | tf_op jit(solution)/shard_map/ppermute | solution.py:22
  41.5 2.6 %collective-permute-start.10 = (f32[1,8,66,1]{3,1,0,2:T(8,128)S(1)}, f32[1,8,66,1]{3,1,0,2:T(8,128)S(1)}, u32[]{:S(2)}, u32[]{:S(2)}) collective-permute-start(f32[1,8,66,1]{3,1,0,2:T(8,128)S(1)} %get-tuple-element.7), channel_id=1, source_target_pairs={{0,1},{2,3},{4,5},{6,7},{8,9},{10,11},{12,13},{14,15},{16,17},{18,... | collective-permute-start | bytes 6344 | tf_op jit(solution)/shard_map/ppermute | solution.py:21
  42.9 3.4 %collective-permute-start.11 = (f32[1,8,66,1]{3,1,0,2:T(8,128)S(1)}, f32[1,8,66,1]{3,1,0,2:T(8,128)S(1)}, u32[]{:S(2)}, u32[]{:S(2)}) collective-permute-start(f32[1,8,66,1]{3,1,0,2:T(8,128)S(1)} %get-tuple-element.8), channel_id=1, source_target_pairs={{1,0},{3,2},{5,4},{7,6},{9,8},{11,10},{13,12},{15,14},{17,16},{19,... | collective-permute-start | bytes 6344 | tf_op jit(solution)/shard_map/ppermute | solution.py:22
  46.7 4.2 %collective-permute-start.12 = (f32[1,8,1,256]{3,1,0,2:T(8,128)S(1)}, f32[1,8,1,256]{3,1,0,2:T(8,128)S(1)}, u32[]{:S(2)}, u32[]{:S(2)}) collective-permute-start(f32[1,8,1,256]{3,1,0,2:T(8,128)S(1)} %get-tuple-element.13), channel_id=1, source_target_pairs={{0,2},{2,4},{4,6},{1,3},{3,5},{5,7},{8,10},{10,12},{12,14},{9,11},... | collective-permute-start | bytes 24584 | tf_op jit(solution)/shard_map/ppermute | solution.py:21
  49.6 5.5 %collective-permute-start.13 = (f32[1,8,1,256]{3,1,0,2:T(8,128)S(1)}, f32[1,8,1,256]{3,1,0,2:T(8,128)S(1)}, u32[]{:S(2)}, u32[]{:S(2)}) collective-permute-start(f32[1,8,1,256]{3,1,0,2:T(8,128)S(1)} %get-tuple-element.14), channel_id=1, source_target_pairs={{2,0},{4,2},{6,4},{3,1},{5,3},{7,5},{10,8},{12,10},{14,12},{11,9},... | collective-permute-start | bytes 24584 | tf_op jit(solution)/shard_map/ppermute | solution.py:22
  55.3 2.6 %collective-permute-start.14 = (f32[1,8,66,1]{3,1,0,2:T(8,128)S(1)}, f32[1,8,66,1]{3,1,0,2:T(8,128)S(1)}, u32[]{:S(2)}, u32[]{:S(2)}) collective-permute-start(f32[1,8,66,1]{3,1,0,2:T(8,128)S(1)} %get-tuple-element.5), channel_id=1, source_target_pairs={{0,1},{2,3},{4,5},{6,7},{8,9},{10,11},{12,13},{14,15},{16,17},{18,... | collective-permute-start | bytes 6344 | tf_op jit(solution)/shard_map/ppermute | solution.py:21
  56.6 3.4 %collective-permute-start.15 = (f32[1,8,66,1]{3,1,0,2:T(8,128)S(1)}, f32[1,8,66,1]{3,1,0,2:T(8,128)S(1)}, u32[]{:S(2)}, u32[]{:S(2)}) collective-permute-start(f32[1,8,66,1]{3,1,0,2:T(8,128)S(1)} %get-tuple-element.6), channel_id=1, source_target_pairs={{1,0},{3,2},{5,4},{7,6},{9,8},{11,10},{13,12},{15,14},{17,16},{19,... | collective-permute-start | bytes 6344 | tf_op jit(solution)/shard_map/ppermute | solution.py:22
  61.2 5.0 %copy-start.5 = (s32[16,2]{0,1:T(2,128)S(1)}, s32[16,2]{0,1:T(2,128)}, u32[]{:S(2)}) copy-start(s32[16,2]{0,1:T(2,128)} %param.13) | copy-start | bytes 388
  61.2 5.2 %copy-start.2 = (f32[16,2,128]{2,1,0:T(2,128)S(1)}, f32[16,2,128]{2,1,0:T(2,128)}, u32[]{:S(2)}) copy-start(f32[16,2,128]{2,1,0:T(2,128)} %param.11) | copy-start | bytes 49156
  61.2 19.8 %all-to-all-start = ((f32[1,8,64,256]{3,1,0,2:T(8,128)}), f32[1,8,64,256]{3,1,0,2:T(8,128)S(1)}, u32[]{:S(2)}, u32[]{:S(2)}) async-start(f32[1,8,64,256]{3,1,0,2:T(8,128)} %fusion.12), calls=%async_computation | async-start | bytes 1048576 | tf_op jit(solution)/shard_map/all_to_all | solution.py:89
  81.8 0.7 copy-start.6
  82.5 7.6 %copy-start.3 = (f32[16,2,128]{2,1,0:T(2,128)S(1)}, f32[16,2,128]{2,1,0:T(2,128)}, u32[]{:S(2)}) copy-start(f32[16,2,128]{2,1,0:T(2,128)} %param.10) | copy-start | bytes 49156
where the time goes:
time: 130 us; the launch traced here: 129 us
  waiting for transfers between devices  39.7 us (31%)
  starting transfers between devices  36 us (28%)
  blocking collectives  16.4 us (13%)
  other arithmetic  15.8 us (12%)
  matrix products  14.4 us (11%)
  local copies, waits for them, and re-layouts  6.36 us (5%)
    ppermute x8, waiting for transfers between devices, extended(): after = lax.ppermute(initial, axis, down)  25 us
    ppermute x8, starting transfers between devices, extended(): before = lax.ppermute(last, axis, up)  20.6 us
    all_to_all x1, blocking collectives, on_device(): lax.all_to_all(returned, 'grp', split_axis=0, concat_axis=2, tiled=True)  16.4 us
    all_to_all x1, waiting for transfers between devices, on_device(): lax.all_to_all(present_state, 'grp', split_axis=2, concat_axis=0, tiled=T...  14.5 us
    another operation x3, other arithmetic, analyse(): factor = jnp.linalg.cholesky(system)  12.2 us
    ppermute x8, starting transfers between devices, extended(): after = lax.ppermute(initial, axis, down)  10.3 us
    dot_general x1, matrix products, on_device(): jnp.einsum('pmc,psc->pms', background, selector, precision=HIGHEST)  7.62 us
    all_to_all x1, starting transfers between devices, on_device(): lax.all_to_all(present_state, 'grp', split_axis=2, concat_axis=0, tiled=T...  5 us
  transfers between devices with their start and end apart: 17, of which 9 were waited for; matrix products, arithmetic and copies ran while one was open for 0% of the time, Pallas kernels for 0%

commit v1 on v0

--- a/solution.py
+++ b/solution.py
@@ -1,6 +1,10 @@
+import functools
+
 import jax
 import jax.numpy as jnp
 from jax import lax
+from jax.experimental import pallas as pl
+from jax.experimental.pallas import tpu as pltpu
 from jax.sharding import PartitionSpec as P
 
 PATCH = 128
@@ -72,7 +76,7 @@
     return centre_mean + jnp.einsum("pki,pkc->pic", combined, perturbed, precision=HIGHEST)
 
 
-def on_device(
+def on_device_plain(
     starting_concentration_per_run,
     diffusivity,
     run_layer_stability_number,
@@ -111,6 +115,425 @@
     return lax.all_to_all(returned, "grp", split_axis=0, concat_axis=2, tiled=True)
 
 
+EDGE = 8
+LANES = 128
+MESH = pl.DeviceIdType.MESH
+
+
+def sym_product(a, b):
+    size = len(a)
+    c = [[None] * size for _ in range(size)]
+    for i in range(size):
+        for j in range(i, size):
+            total = a[i][0] * b[0][j]
+            for k in range(1, size):
+                total = total + a[i][k] * b[k][j]
+            c[i][j] = c[j][i] = total
+    return c
+
+
+def weights(system, source):
+    size = len(system)
+    low = [[None] * size for _ in range(size)]
+    for j in range(size):
+        diag = system[j][j]
+        for k in range(j):
+            diag = diag - low[j][k] * low[j][k]
+        low[j][j] = jnp.sqrt(diag)
+        for i in range(j + 1, size):
+            v = system[i][j]
+            for k in range(j):
+                v = v - low[i][k] * low[j][k]
+            low[i][j] = v / low[j][j]
+    half = []
+    for i in range(size):
+        v = source[i]
+        for k in range(i):
+            v = v - low[i][k] * half[k]
+        half.append(v / low[i][i])
+    mean_weight = [None] * size
+    for i in reversed(range(size)):
+        v = half[i]
+        for k in range(i + 1, size):
+            v = v - low[k][i] * mean_weight[k]
+        mean_weight[i] = v / low[i][i]
+    total = None
+    for i in range(size):
+        for j in range(size):
+            sq = system[i][j] * system[i][j]
+            total = sq if total is None else total + sq
+    norm_scale = jnp.sqrt(total)
+    iterate = [[None] * size for _ in range(size)]
+    for i in range(size):
+        for j in range(i, size):
+            iterate[i][j] = iterate[j][i] = system[i][j] / norm_scale
+    root = None
+    for sweep in range(NS_ITERS):
+        prod = iterate if root is None else sym_product(root, iterate)
+        update = [[None] * size for _ in range(size)]
+        for i in range(size):
+            for j in range(i, size):
+                v = -0.5 * prod[i][j]
+                update[i][j] = update[j][i] = 1.5 + v if i == j else v
+        if sweep < NS_ITERS - 1:
+            iterate = sym_product(iterate, update)
+        root = update if root is None else sym_product(update, root)
+    scale = jnp.sqrt((size - 1.0) / norm_scale)
+    return [[root[k][i] * scale + mean_weight[k] for i in range(size)] for k in range(size)]
+
+
+def kernel(
+    sizes, x_ref, d_ref, wind, obs, var, site, count, out,
+    field, inside, made, ground, result, up_send, down_send, up_recv, down_recv,
+    cols_send, cols_recv, load_sem, halo_send, halo_recv, ens_send, ens_recv, back_send, back_recv, own_sem,
+):
+    groups, subs, levels, high, wide, band, patches = sizes
+    me, mine, core = lax.axis_index("grp"), lax.axis_index("sub"), lax.axis_index("rep")
+    other = 1 - core
+    tall, across = high + 2 * EDGE, wide + LANES
+    has_up, has_down = mine > 0, mine < subs - 1
+    loads = [
+        pltpu.make_async_copy(x_ref, field.at[pl.ds(0, levels), pl.ds(EDGE, high), pl.ds(0, wide)], load_sem.at[0]),
+        pltpu.make_async_copy(d_ref, field.at[levels, pl.ds(EDGE, high), pl.ds(0, wide)], load_sem.at[1]),
+    ]
+    for c in loads:
+        c.start()
+
+    barrier = pltpu.get_barrier_semaphore()
+    for step in range(1, groups):
+        peer = lax.rem(me + step, groups)
+        pl.semaphore_signal(barrier, inc=1, device_id={"grp": peer}, device_id_type=MESH)
+    pl.semaphore_signal(barrier, inc=1, device_id={"rep": other}, device_id_type=MESH)
+
+    @pl.when(has_up)
+    def _():
+        pl.semaphore_signal(barrier, inc=1, device_id={"sub": mine - 1}, device_id_type=MESH)
+        pl.semaphore_signal(barrier, inc=1, device_id={"sub": mine - 1, "rep": other}, device_id_type=MESH)
+
+    @pl.when(has_down)
+    def _():
+        pl.semaphore_signal(barrier, inc=1, device_id={"sub": mine + 1}, device_id_type=MESH)
+        pl.semaphore_signal(barrier, inc=1, device_id={"sub": mine + 1, "rep": other}, device_id_type=MESH)
+
+    row = lax.broadcasted_iota(jnp.int32, (tall, across), 0) - EDGE
+    col = lax.broadcasted_iota(jnp.int32, (tall, across), 1)
+    row_ok = ((row >= 0) | has_up) & ((row < high) | has_down)
+    row_ok = row_ok & (row >= -STEPS) & (row < high + STEPS)
+    col_ok = (col < wide) | ((col < wide + STEPS) & (core == 0)) | ((col >= across - STEPS) & (core > 0))
+    inside[...] = jnp.where(row_ok & col_ok, 1.0, 0.0)
+
+    for c in loads:
+        c.wait()
+
+    fields = levels + 1
+    lane = lax.broadcasted_iota(jnp.int32, (high, LANES), 1)
+    slot_of_lane = lax.rem(lane + STEPS, LANES) // (2 * STEPS)
+    packed = jnp.zeros((high, LANES), jnp.float32)
+    for f in range(fields):
+        inner = field[f, EDGE : EDGE + high, wide - LANES : wide]
+        outer = field[f, EDGE : EDGE + high, 0:LANES]
+        tile = jnp.where(core == 0, inner, outer)
+        if f:
+            tile = pltpu.roll(tile, 2 * STEPS * f, 1)
+        packed = jnp.where(slot_of_lane == f, tile, packed)
+    cols_send[...] = packed
+    sub_row = lax.broadcasted_iota(jnp.int32, (EDGE, wide), 0)
+    for k in range((fields + 1) // 2):
+        a, b = 2 * k, min(2 * k + 1, fields - 1)
+        top_a, top_b = field[a, EDGE : 2 * EDGE, 0:wide], field[b, EDGE : 2 * EDGE, 0:wide]
+        low_a, low_b = field[a, high : high + EDGE, 0:wide], field[b, high : high + EDGE, 0:wide]
+        up_send[k] = jnp.where(sub_row < STEPS, top_a, pltpu.roll(top_b, STEPS, 0))
+        down_send[k] = jnp.where(sub_row >= STEPS, low_a, pltpu.roll(low_b, STEPS, 0))
+
+    pl.semaphore_wait(
+        barrier, groups + 2 * has_up.astype(jnp.int32) + 2 * has_down.astype(jnp.int32)
+    )
+
+    def halo(src, dst, n, device):
+        return pltpu.make_async_remote_copy(
+            src_ref=src, dst_ref=dst, send_sem=halo_send.at[n], recv_sem=halo_recv.at[n],
+            device_id=device, device_id_type=MESH,
+        )
+
+    beside = halo(cols_send, cols_recv.at[pl.ds(EDGE, high)], 0, {"rep": other})
+    beside.start()
+    upward = [
+        halo(up_send, down_recv, 1, {"sub": mine - 1}),
+        halo(cols_send.at[pl.ds(0, EDGE)], cols_recv.at[pl.ds(EDGE + high, EDGE)], 2, {"sub": mine - 1, "rep": other}),
+    ]
+    downward = [
+        halo(down_send, up_recv, 3, {"sub": mine + 1}),
+        halo(cols_send.at[pl.ds(high - EDGE, EDGE)], cols_recv.at[pl.ds(0, EDGE)], 4, {"sub": mine + 1, "rep": other}),
+    ]
+
+    @pl.when(has_up)
+    def _():
+        for c in upward:
+            c.start()
+
+    @pl.when(has_down)
+    def _():
+        for c in downward:
+            c.start()
+
+    beside.wait_recv()
+
+    def place_columns(first, rows):
+        got = cols_recv[first : first + rows]
+        ok = inside[first : first + rows, wide:across] > 0.0
+        for f in range(fields):
+            tile = pltpu.roll(got, LANES - 2 * STEPS * f, 1) if f else got
+            field[f, first : first + rows, wide:across] = jnp.where(ok, tile, 0.0)
+
+    place_columns(EDGE, high)
+
+    def forecast(level, first, rows):
+        q = field[level, first : first + rows]
+        d = field[levels, first : first + rows]
+        wind_here = inside[first : first + rows] * wind[0, level]
+        for _ in range(STEPS):
+            west = pltpu.roll(q, 1, 1)
+            east = pltpu.roll(q, across - 1, 1)
+            north = pltpu.roll(q, 1, 0)
+            south = pltpu.roll(q, rows - 1, 0)
+            spread = (north + south) + (west + east) - 4.0 * q
+            q = q + d * spread - wind_here * (q - west)
+        return q[EDGE : rows - EDGE, 0:wide]
+
+    def ensemble(level, target, owner):
+        return pltpu.make_async_remote_copy(
+            src_ref=made.at[level, pl.ds(target * band, band)],
+            dst_ref=ground.at[owner, level],
+            send_sem=ens_send.at[target], recv_sem=ens_recv.at[owner],
+            device_id={"grp": target}, device_id_type=MESH,
+        )
+
+    def send_band(level, target):
+        @pl.when(me != target)
+        def _():
+            ensemble(level, target, me).start()
+
+    def middle(level, carry):
+        made[level, band : high - band] = forecast(level, band, high - 2 * band + 2 * EDGE)
+        for target in range(1, groups - 1):
+            send_band(level, target)
+        return carry
+
+    lax.fori_loop(0, levels, middle, 0)
+
+    @pl.when(has_up)
+    def _():
+        for c in downward:
+            c.wait_recv()
+
+    @pl.when(has_down)
+    def _():
+        for c in upward:
+            c.wait_recv()
+
+    place_columns(0, EDGE)
+    place_columns(EDGE + high, EDGE)
+    for f in range(fields):
+        above, below = up_recv[f // 2], down_recv[f // 2]
+        if f % 2:
+            above, below = pltpu.roll(above, STEPS, 0), pltpu.roll(below, STEPS, 0)
+        field[f, 0:EDGE, 0:wide] = jnp.where(inside[0:EDGE, 0:wide] > 0.0, above, 0.0)
+        field[f, EDGE + high : tall, 0:wide] = jnp.where(inside[EDGE + high : tall, 0:wide] > 0.0, below, 0.0)
+
+    def outer_bands(level, carry):
+        made[level, 0:band] = forecast(level, 0, band + 2 * EDGE)
+        send_band(level, 0)
+        made[level, high - band : high] = forecast(level, high - band, band + 2 * EDGE)
+        send_band(level, groups - 1)
+        return carry
+
+    lax.fori_loop(0, levels, outer_bands, 0)
+    ground[me] = made[:, pl.ds(pl.multiple_of(me * band, band), band), :]
+
+    def whole_band(target, owner):
+        return pltpu.make_async_remote_copy(
+            src_ref=made.at[:, pl.ds(target * band, band)],
+            dst_ref=ground.at[owner],
+            send_sem=ens_send.at[target], recv_sem=ens_recv.at[owner],
+            device_id={"grp": target}, device_id_type=MESH,
+        )
+
+    for step in range(1, groups):
+        peer = lax.rem(me + step, groups)
+        whole_band(peer, peer).wait_recv()
+
+    patch = wide // patches
+    tiles = [(h, p) for h in range(band // EDGE) for p in range(patches)]
+    shape = (EDGE, LANES)
+    lanes = lax.broadcasted_iota(jnp.int32, shape, 1)
+    system = [[None] * groups for _ in range(groups)]
+    source = [None] * groups
+
+    def put(old, new, index):
+        new = jnp.broadcast_to(new, shape)
+        return new if old is None else jnp.where(lanes == index, new, old)
+
+    for index, (h, p) in enumerate(tiles):
+        rows = slice(h * EDGE, (h + 1) * EDGE)
+        here = site[rows, p, :]
+        level_of, col_of = here // patch, lax.rem(here, patch)
+        sampled = []
+        for m in range(groups):
+            got = jnp.zeros(shape, jnp.float32)
+            for l in range(levels):
+                tile = ground[m, l, rows, p * patch : (p + 1) * patch]
+                pick = jnp.take_along_axis(tile, col_of, axis=1, mode="promise_in_bounds")
+                got = jnp.where(level_of == l, pick, got)
+            sampled.append(got)
+        mean = sum(sampled[1:], sampled[0]) * (1.0 / groups)
+        pert = [s - mean for s in sampled]
+        precision = jnp.where(lanes < count[rows, p : p + 1], 1.0 / var[rows, p, :], 0.0)
+        innovation = obs[rows, p, :] - mean
+        for i in range(groups):
+            weighted = pert[i] * precision
+            source[i] = put(source[i], jnp.sum(weighted * innovation, axis=1, keepdims=True), index)
+            for j in range(i, groups):
+                v = jnp.sum(weighted * pert[j], axis=1, keepdims=True)
+                v = v + (groups - 1.0) if i == j else v
+                system[i][j] = system[j][i] = put(system[i][j], v, index)
+    combined = weights(system, source)
+
+    def back(h, target, owner):
+        return pltpu.make_async_remote_copy(
+            src_ref=result.at[target, :, pl.ds(h * EDGE, EDGE)],
+            dst_ref=out.at[:, pl.ds(owner * band + h * EDGE, EDGE)],
+            send_sem=back_send.at[target], recv_sem=back_recv.at[owner],
+            device_id={"grp": target}, device_id_type=MESH,
+        )
+
+    for h in range(band // EDGE):
+        rows = slice(h * EDGE, (h + 1) * EDGE)
+        for p in range(patches):
+            index = h * patches + p
+            c = [
+                [jnp.broadcast_to(combined[k][i][:, index : index + 1], shape) for i in range(groups)]
+                for k in range(groups)
+            ]
+            cells = slice(p * patch, (p + 1) * patch)
+            for l in range(levels):
+                member = [ground[m, l, rows, cells] for m in range(groups)]
+                mean = sum(member[1:], member[0]) * (1.0 / groups)
+                pert = [v - mean for v in member]
+                for i in range(groups):
+                    v = c[0][i] * pert[0]
+                    for k in range(1, groups):
+                        v = v + c[k][i] * pert[k]
+                    result[i, l, rows, cells] = mean + v
+        for step in range(1, groups):
+            peer = lax.rem(me + step, groups)
+            back(h, peer, me).start()
+    own = pltpu.make_async_copy(result.at[me], out.at[:, pl.ds(me * band, band)], own_sem)
+    own.start()
+
+    beside.wait_send()
+
+    @pl.when(has_up)
+    def _():
+        for c in upward:
+            c.wait_send()
+
+    @pl.when(has_down)
+    def _():
+        for c in downward:
+            c.wait_send()
+
+    def whole_back(target, owner):
+        return pltpu.make_async_remote_copy(
+            src_ref=result.at[target],
+            dst_ref=out.at[:, pl.ds(owner * band, band)],
+            send_sem=back_send.at[target], recv_sem=back_recv.at[owner],
+            device_id={"grp": target}, device_id_type=MESH,
+        )
+
+    for step in range(1, groups):
+        peer = lax.rem(me + step, groups)
+        whole_band(peer, me).wait_send()
+        whole_back(peer, me).wait_send()
+        whole_back(peer, peer).wait_recv()
+    own.wait()
+
+
+def fused(state, diffusivity, wind, observed, variance, site, count):
+    groups, subs = lax.axis_size("grp"), lax.axis_size("sub")
+    _, levels, high, wide = state.shape
+    band, patches, _ = observed.shape
+    tall, across = high + 2 * EDGE, wide + LANES
+    pairs = (levels + 2) // 2
+    f32 = jnp.float32
+    vmem, dma = pltpu.VMEM, pltpu.SemaphoreType.DMA
+    whole = pl.BlockSpec(memory_space=pltpu.VMEM)
+    anywhere = pl.BlockSpec(memory_space=pl.ANY)
+    sizes = (groups, subs, levels, high, wide, band, patches)
+    out = pl.pallas_call(
+        functools.partial(kernel, sizes),
+        out_shape=jax.ShapeDtypeStruct((levels, high, wide), f32),
+        in_specs=[anywhere, anywhere, pl.BlockSpec(memory_space=pltpu.SMEM), whole, whole, whole, whole],
+        out_specs=anywhere,
+        scratch_shapes=[
+            vmem((levels + 1, tall, across), f32),
+            vmem((tall, across), f32),
+            vmem((levels, high, wide), f32),
+            vmem((groups, levels, band, wide), f32),
+            vmem((groups, levels, band, wide), f32),
+            vmem((pairs, EDGE, wide), f32),
+            vmem((pairs, EDGE, wide), f32),
+            vmem((pairs, EDGE, wide), f32),
+            vmem((pairs, EDGE, wide), f32),
+            vmem((high, LANES), f32),
+            vmem((tall, LANES), f32),
+            dma((2,)),
+            dma((5,)),
+            dma((5,)),
+            dma((groups,)),
+            dma((groups,)),
+            dma((groups,)),
+            dma((groups,)),
+            dma(()),
+        ],
+        compiler_params=pltpu.CompilerParams(collective_id=0, has_side_effects=True),
+    )(state[0], diffusivity, wind, observed, variance, site, count)
+    return out[None]
+
+
+def on_device(
+    starting_concentration_per_run,
+    diffusivity,
+    run_layer_stability_number,
+    observed,
+    slot_error_variance,
+    sensor_target_site,
+    patch_live_count,
+):
+    groups, subs, reps = lax.axis_size("grp"), lax.axis_size("sub"), lax.axis_size("rep")
+    members, levels, high, wide = starting_concentration_per_run.shape
+    band, patches, slots = observed.shape
+    fits = (
+        members == 1
+        and reps == 2
+        and 3 <= groups <= 8
+        and subs >= 2
+        and band % EDGE == 0
+        and 2 * STEPS * (levels + 1) <= LANES
+        and wide == patches * PATCH
+        and PATCH == LANES == slots
+    )
+    step = fused if fits else on_device_plain
+    return step(
+        starting_concentration_per_run,
+        diffusivity,
+        run_layer_stability_number,
+        observed,
+        slot_error_variance,
+        sensor_target_site,
+        patch_live_count,
+    )
+
+
 def solution(mesh):
     in_specs = (
         P("grp", None, "sub", "rep"),

time: 130 us -> 36.5 us (0.28)
  waiting for transfers between devices: 39.7 us -> 0 us
  starting transfers between devices: 36 us -> 0 us
  Pallas kernels: 0 us -> 33 us
  blocking collectives: 16.4 us -> 0 us
  other arithmetic: 15.8 us -> 0 us
  matrix products: 14.4 us -> 0 us
  local copies, waits for them, and re-layouts: 6.36 us -> 3.23 us
    pallas_call x0 -> x1, Pallas kernels: none -> 33 us  [fused(): pl.pallas_call(functools.partial(kernel, sizes), out_shape=jax.ShapeDtype...]
    ppermute x16 -> x0, starting transfers between devices: 31 us -> none  [the longest x8 20.6 us: extended(): before = lax.ppermute(last, axis, up)]
    ppermute x16 -> x0, waiting for transfers between devices: 25.2 us -> none  [the longest x8 25 us: extended(): after = lax.ppermute(initial, axis, down)]
    all_to_all x1 -> x0, blocking collectives: 16.4 us -> none  [on_device(): lax.all_to_all(returned, 'grp', split_axis=0, concat_axis=2, tiled=True)]
    all_to_all x1 -> x0, waiting for transfers between devices: 14.5 us -> none  [on_device(): lax.all_to_all(present_state, 'grp', split_axis=2, concat_axis=0, tiled=T...]
    dot_general x15 -> x0, matrix products: 13.7 us -> none  [the longest x1 7.62 us: on_device(): jnp.einsum('pmc,psc->pms', background, selector, precision=HIGHEST)]
    another operation x6 -> x0, other arithmetic: 12.7 us -> none  [the longest x3 12.2 us: analyse(): factor = jnp.linalg.cholesky(system)]
    all_to_all x1 -> x0, starting transfers between devices: 5 us -> none  [on_device(): lax.all_to_all(present_state, 'grp', split_axis=2, concat_axis=0, tiled=T...]
  transfers between devices with their start and end apart: 17 -> 0, of which waited for: 9 -> 0; matrix products, arithmetic and copies ran while one was open for 0% -> 0% of each run, Pallas kernels for 0% -> 0%
where the time goes in v1:
time: 36.5 us; the launch traced here: 36.3 us
  Pallas kernels  33 us (90%)
  local copies, waits for them, and re-layouts  3.23 us (9%)
    pallas_call x1, Pallas kernels, fused(): pl.pallas_call(functools.partial(kernel, sizes), out_shape=jax.ShapeDtype...  33 us
    unnamed x4, local copies, waits for them, and re-layouts  3.23 us

profile of v1, /device:TPU:0, one launch (start us, length us, event | category | flops | bytes accessed | tf_op | source)
XLA Modules:
  0.0 36.3 jit_solution(12048967232417518454)
XLA Ops:
  0.0 0.0 copy-start
  0.0 0.7 %copy-done = s32[16,2]{0,1:T(2,128)S(1)} copy-done((s32[16,2]{0,1:T(2,128)S(1)}, s32[16,2]{0,1:T(2,128)}, u32[]{:S(2)}) %copy-start) | copy-done | bytes 152
  0.7 0.7 %copy.8.count = s32[16,2]{1,0:T(8,128)} copy(s32[16,2]{0,1:T(2,128)S(1)} %copy-done) | data formatting | bytes 256 | tf_op args[6]
  1.4 33.0 %shard_map.73 = f32[8,64,256]{2,1,0:T(8,128)} custom-call(f32[8,64,256]{2,1,0:T(8,128)} %bitcast.3, f32[64,256]{1,0:T(8,128)} %d_ref.1, f32[1,8]{1,0:T(1,128)} %wind.1, f32[16,2,128]{2,1,0:T(2,128)} %obs.1, f32[16,2,128]{2,1,0:T(2,128)} %var.1, s32[16,2,128]{2,1,0:T(2,128)} %site.1, s32[16,2]{1,0:T(8,128)} %copy.8.count), custom_call_target="tpu_custom_call" | custom-call | tf_op jit(solution)/shard_map/pallas_call | solution.py:472
  34.4 1.9 %copy.10 = f32[1,8,64,256]{3,2,1,0:T(8,128)} copy(f32[1,8,64,256]{3,2,1,0:T(8,128)} %bitcast.2) | data formatting | bytes 1048576
Async XLA Ops:
  0.0 0.7 %copy-start = (s32[16,2]{0,1:T(2,128)S(1)}, s32[16,2]{0,1:T(2,128)}, u32[]{:S(2)}) copy-start(s32[16,2]{0,1:T(2,128)} %param.13) | copy-start | bytes 388

commit v2 on v1

--- a/solution.py
+++ b/solution.py
@@ -116,6 +116,7 @@
 
 
 EDGE = 8
+SCOPED = 24 * 1024 * 1024
 LANES = 128
 MESH = pl.DeviceIdType.MESH
 
@@ -183,7 +184,8 @@
 
 
 def kernel(
-    sizes, x_ref, d_ref, wind, obs, var, site, count, out,
+    sizes, x_ref, d_ref, wind_ref, obs_ref, var_ref, site_ref, count_ref, out,
+    wind, count, obs, var, site,
     field, inside, made, ground, result, up_send, down_send, up_recv, down_recv,
     cols_send, cols_recv, load_sem, halo_send, halo_recv, ens_send, ens_recv, back_send, back_recv, own_sem,
 ):
@@ -195,8 +197,15 @@
     loads = [
         pltpu.make_async_copy(x_ref, field.at[pl.ds(0, levels), pl.ds(EDGE, high), pl.ds(0, wide)], load_sem.at[0]),
         pltpu.make_async_copy(d_ref, field.at[levels, pl.ds(EDGE, high), pl.ds(0, wide)], load_sem.at[1]),
+        pltpu.make_async_copy(wind_ref, wind, load_sem.at[2]),
     ]
-    for c in loads:
+    late_loads = [
+        pltpu.make_async_copy(obs_ref, obs, load_sem.at[3]),
+        pltpu.make_async_copy(var_ref, var, load_sem.at[4]),
+        pltpu.make_async_copy(site_ref, site, load_sem.at[5]),
+        pltpu.make_async_copy(count_ref, count, load_sem.at[6]),
+    ]
+    for c in loads + late_loads:
         c.start()
 
     barrier = pltpu.get_barrier_semaphore()
@@ -222,6 +231,7 @@
     col_ok = (col < wide) | ((col < wide + STEPS) & (core == 0)) | ((col >= across - STEPS) & (core > 0))
     inside[...] = jnp.where(row_ok & col_ok, 1.0, 0.0)
 
+    field[:, :, wide:across] = jnp.zeros((levels + 1, tall, LANES), jnp.float32)
     for c in loads:
         c.wait()
 
@@ -276,16 +286,12 @@
         for c in downward:
             c.start()
 
-    beside.wait_recv()
-
     def place_columns(first, rows):
         got = cols_recv[first : first + rows]
         ok = inside[first : first + rows, wide:across] > 0.0
         for f in range(fields):
             tile = pltpu.roll(got, LANES - 2 * STEPS * f, 1) if f else got
             field[f, first : first + rows, wide:across] = jnp.where(ok, tile, 0.0)
-
-    place_columns(EDGE, high)
 
     def forecast(level, first, rows):
         q = field[level, first : first + rows]
@@ -300,26 +306,36 @@
             q = q + d * spread - wind_here * (q - west)
         return q[EDGE : rows - EDGE, 0:wide]
 
-    def ensemble(level, target, owner):
+    def ensemble(level, target, owner, cells):
         return pltpu.make_async_remote_copy(
-            src_ref=made.at[level, pl.ds(target * band, band)],
-            dst_ref=ground.at[owner, level],
+            src_ref=made.at[level, pl.ds(target * band, band), cells],
+            dst_ref=ground.at[owner, level, :, cells],
             send_sem=ens_send.at[target], recv_sem=ens_recv.at[owner],
             device_id={"grp": target}, device_id_type=MESH,
         )
 
-    def send_band(level, target):
+    def send_band(level, target, cells):
         @pl.when(me != target)
         def _():
-            ensemble(level, target, me).start()
-
-    def middle(level, carry):
-        made[level, band : high - band] = forecast(level, band, high - 2 * band + 2 * EDGE)
+            ensemble(level, target, me, cells).start()
+
+    def middle(cells, left, right, level, carry):
+        new = forecast(level, band, high - 2 * band + 2 * EDGE)
+        made[level, band : high - band, cells] = jnp.where(core == 0, new[:, left], new[:, right])
         for target in range(1, groups - 1):
-            send_band(level, target)
+            send_band(level, target, cells)
         return carry
 
-    lax.fori_loop(0, levels, middle, 0)
+    far = pl.ds(pl.multiple_of(core * LANES, LANES), wide - LANES)
+    near = pl.ds(pl.multiple_of((1 - core) * (wide - LANES), LANES), LANES)
+    lax.fori_loop(
+        0, levels, functools.partial(middle, far, slice(0, wide - LANES), slice(LANES, wide)), 0
+    )
+    beside.wait_recv()
+    place_columns(EDGE, high)
+    lax.fori_loop(
+        0, levels, functools.partial(middle, near, slice(wide - LANES, wide), slice(0, LANES)), 0
+    )
 
     @pl.when(has_up)
     def _():
@@ -342,9 +358,9 @@
 
     def outer_bands(level, carry):
         made[level, 0:band] = forecast(level, 0, band + 2 * EDGE)
-        send_band(level, 0)
+        send_band(level, 0, pl.ds(0, wide))
         made[level, high - band : high] = forecast(level, high - band, band + 2 * EDGE)
-        send_band(level, groups - 1)
+        send_band(level, groups - 1, pl.ds(0, wide))
         return carry
 
     lax.fori_loop(0, levels, outer_bands, 0)
@@ -362,10 +378,13 @@
         peer = lax.rem(me + step, groups)
         whole_band(peer, peer).wait_recv()
 
+    for c in late_loads:
+        c.wait()
     patch = wide // patches
     tiles = [(h, p) for h in range(band // EDGE) for p in range(patches)]
     shape = (EDGE, LANES)
     lanes = lax.broadcasted_iota(jnp.int32, shape, 1)
+    sub_lines = lax.broadcasted_iota(jnp.int32, shape, 0)
     system = [[None] * groups for _ in range(groups)]
     source = [None] * groups
 
@@ -387,7 +406,10 @@
             sampled.append(got)
         mean = sum(sampled[1:], sampled[0]) * (1.0 / groups)
         pert = [s - mean for s in sampled]
-        precision = jnp.where(lanes < count[rows, p : p + 1], 1.0 / var[rows, p, :], 0.0)
+        live = jnp.zeros(shape, jnp.int32)
+        for r in range(EDGE):
+            live = jnp.where(sub_lines == r, count[p, h * EDGE + r], live)
+        precision = jnp.where(lanes < live, 1.0 / var[rows, p, :], 0.0)
         innovation = obs[rows, p, :] - mean
         for i in range(groups):
             weighted = pert[i] * precision
@@ -466,15 +488,20 @@
     pairs = (levels + 2) // 2
     f32 = jnp.float32
     vmem, dma = pltpu.VMEM, pltpu.SemaphoreType.DMA
-    whole = pl.BlockSpec(memory_space=pltpu.VMEM)
+    in_hbm = pl.BlockSpec(memory_space=pltpu.HBM)
     anywhere = pl.BlockSpec(memory_space=pl.ANY)
     sizes = (groups, subs, levels, high, wide, band, patches)
     out = pl.pallas_call(
         functools.partial(kernel, sizes),
         out_shape=jax.ShapeDtypeStruct((levels, high, wide), f32),
-        in_specs=[anywhere, anywhere, pl.BlockSpec(memory_space=pltpu.SMEM), whole, whole, whole, whole],
+        in_specs=[in_hbm] * 7,
         out_specs=anywhere,
         scratch_shapes=[
+            pltpu.SMEM(wind.shape, f32),
+            pltpu.SMEM(count.shape[::-1], jnp.int32),
+            vmem(observed.shape, f32),
+            vmem(observed.shape, f32),
+            vmem(observed.shape, jnp.int32),
             vmem((levels + 1, tall, across), f32),
             vmem((tall, across), f32),
             vmem((levels, high, wide), f32),
@@ -486,7 +513,7 @@
             vmem((pairs, EDGE, wide), f32),
             vmem((high, LANES), f32),
             vmem((tall, LANES), f32),
-            dma((2,)),
+            dma((7,)),
             dma((5,)),
             dma((5,)),
             dma((groups,)),
@@ -495,8 +522,11 @@
             dma((groups,)),
             dma(()),
         ],
-        compiler_params=pltpu.CompilerParams(collective_id=0, has_side_effects=True),
-    )(state[0], diffusivity, wind, observed, variance, site, count)
+        compiler_params=pltpu.CompilerParams(collective_id=0, has_side_effects=True, vmem_limit_bytes=SCOPED),
+    )(*[
+        pltpu.with_memory_space_constraint(v, pltpu.HBM)
+        for v in (state[0], diffusivity, wind, observed, variance, site, count.T)
+    ])
     return out[None]
 
 

time: 36.5 us -> 35.6 us (0.975)
  local copies, waits for them, and re-layouts: 3.23 us -> 0.8 us
  Pallas kernels: 33 us -> 34.7 us
    unnamed x4 -> x1, local copies, waits for them, and re-layouts: 3.23 us -> 0.8 us
    pallas_call x1, Pallas kernels: 33 us -> 34.7 us  [fused(): pl.pallas_call(functools.partial(kernel, sizes), out_shape=jax.ShapeDtype...]
where the time goes in v2:
time: 35.6 us; the launch traced here: 35.5 us
  Pallas kernels  34.7 us (97%)
  local copies, waits for them, and re-layouts  0.8 us (2%)
    pallas_call x1, Pallas kernels, fused(): pl.pallas_call(functools.partial(kernel, sizes), out_shape=jax.ShapeDtype...  34.7 us
    unnamed x1, local copies, waits for them, and re-layouts  0.8 us

profile of v2, /device:TPU:0, one launch (start us, length us, event | category | flops | bytes accessed | tf_op | source)
XLA Modules:
  0.0 35.5 jit_solution(3612406753611733476)
XLA Ops:
  0.0 34.7 %shard_map.73 = f32[8,64,256]{2,1,0:T(8,128)S(1)} custom-call(f32[8,64,256]{2,1,0:T(8,128)} %bitcast.4, f32[64,256]{1,0:T(8,128)} %d_ref.1, f32[1,8]{1,0:T(1,128)} %wind_ref.1, f32[16,2,128]{2,1,0:T(2,128)} %obs_ref.1, f32[16,2,128]{2,1,0:T(2,128)} %var_ref.1, s32[16,2,128]{2,1,0:T(2,128)} %site_ref.1, s32[2,16]{1,0:T(2,128)} %bitcast.5), custom_call_target="tpu_custom_call" | custom-call | tf_op jit(solution)/shard_map/pallas_call | solution.py:494
  34.7 0.8 %copy.9 = f32[1,8,64,256]{3,2,1,0:T(8,128)} copy(f32[1,8,64,256]{3,2,1,0:T(8,128)S(1)} %bitcast.3) | data formatting | bytes 1048576

commit v3 on v2

--- a/solution.py
+++ b/solution.py
@@ -306,24 +306,26 @@
             q = q + d * spread - wind_here * (q - west)
         return q[EDGE : rows - EDGE, 0:wide]
 
-    def ensemble(level, target, owner, cells):
+    def ensemble(level, target, owner, first, rows, cells):
         return pltpu.make_async_remote_copy(
-            src_ref=made.at[level, pl.ds(target * band, band), cells],
-            dst_ref=ground.at[owner, level, :, cells],
+            src_ref=made.at[level, pl.ds(target * band + first, rows), cells],
+            dst_ref=ground.at[owner, level, pl.ds(first, rows), cells],
             send_sem=ens_send.at[target], recv_sem=ens_recv.at[owner],
             device_id={"grp": target}, device_id_type=MESH,
         )
 
-    def send_band(level, target, cells):
+    def send_band(level, target, first, rows, cells):
         @pl.when(me != target)
         def _():
-            ensemble(level, target, me, cells).start()
+            ensemble(level, target, me, first, rows, cells).start()
 
     def middle(cells, left, right, level, carry):
-        new = forecast(level, band, high - 2 * band + 2 * EDGE)
-        made[level, band : high - band, cells] = jnp.where(core == 0, new[:, left], new[:, right])
+        new = forecast(level, EDGE, high)
+        made[level, EDGE : high - EDGE, cells] = jnp.where(core == 0, new[:, left], new[:, right])
+        send_band(level, 0, EDGE, band - EDGE, cells)
+        send_band(level, groups - 1, 0, band - EDGE, cells)
         for target in range(1, groups - 1):
-            send_band(level, target, cells)
+            send_band(level, target, 0, band, cells)
         return carry
 
     far = pl.ds(pl.multiple_of(core * LANES, LANES), wide - LANES)
@@ -357,10 +359,10 @@
         field[f, EDGE + high : tall, 0:wide] = jnp.where(inside[EDGE + high : tall, 0:wide] > 0.0, below, 0.0)
 
     def outer_bands(level, carry):
-        made[level, 0:band] = forecast(level, 0, band + 2 * EDGE)
-        send_band(level, 0, pl.ds(0, wide))
-        made[level, high - band : high] = forecast(level, high - band, band + 2 * EDGE)
-        send_band(level, groups - 1, pl.ds(0, wide))
+        made[level, 0:EDGE] = forecast(level, 0, 3 * EDGE)
+        send_band(level, 0, 0, EDGE, pl.ds(0, wide))
+        made[level, high - EDGE : high] = forecast(level, high - EDGE, 3 * EDGE)
+        send_band(level, groups - 1, band - EDGE, EDGE, pl.ds(0, wide))
         return carry
 
     lax.fori_loop(0, levels, outer_bands, 0)
@@ -548,6 +550,7 @@
         and 3 <= groups <= 8
         and subs >= 2
         and band % EDGE == 0
+        and band >= 2 * EDGE
         and 2 * STEPS * (levels + 1) <= LANES
         and wide == patches * PATCH
         and PATCH == LANES == slots

time: 35.6 us -> 32.4 us (0.910)
  Pallas kernels: 34.7 us -> 31.4 us
    pallas_call x1, Pallas kernels: 34.7 us -> 31.4 us  [fused(): pl.pallas_call(functools.partial(kernel, sizes), out_shape=jax.ShapeDtype...]
where the time goes in v3:
time: 32.4 us; the launch traced here: 32.2 us
  Pallas kernels  31.4 us (97%)
  local copies, waits for them, and re-layouts  0.8 us (2%)
    pallas_call x1, Pallas kernels, fused(): pl.pallas_call(functools.partial(kernel, sizes), out_shape=jax.ShapeDtype...  31.4 us
    unnamed x1, local copies, waits for them, and re-layouts  0.8 us

profile of v3, /device:TPU:0, one launch (start us, length us, event | category | flops | bytes accessed | tf_op | source)
XLA Modules:
  0.0 32.2 jit_solution(6987673786981926632)
XLA Ops:
  0.0 31.4 %shard_map.73 = f32[8,64,256]{2,1,0:T(8,128)S(1)} custom-call(f32[8,64,256]{2,1,0:T(8,128)} %bitcast.4, f32[64,256]{1,0:T(8,128)} %d_ref.1, f32[1,8]{1,0:T(1,128)} %wind_ref.1, f32[16,2,128]{2,1,0:T(2,128)} %obs_ref.1, f32[16,2,128]{2,1,0:T(2,128)} %var_ref.1, s32[16,2,128]{2,1,0:T(2,128)} %site_ref.1, s32[2,16]{1,0:T(2,128)} %bitcast.5), custom_call_target="tpu_custom_call" | custom-call | tf_op jit(solution)/shard_map/pallas_call | solution.py:496
  31.4 0.8 %copy.9 = f32[1,8,64,256]{3,2,1,0:T(8,128)} copy(f32[1,8,64,256]{3,2,1,0:T(8,128)S(1)} %bitcast.3) | data formatting | bytes 1048576
